TPU v7x, 32 devices: a whole 2x2x4 slice. The times are simulated.
32 devices in a mesh: dp: 2 (over core), cent: 16 (over z, y, x).
Axes of the slice: x: 2, y: 2, z: 4, core: 2. Of those that a mesh axis runs over, the one named last changes fastest.
Arguments:
- embeddings: bfloat16 [4096, 768], P(('dp', 'cent')), may hold values from -20 to 20
- fine_centroids: float32 [8192, 768], P('cent'), may hold values from -8 to 8
- parents: int32 [8192], P('cent'), may hold values from 0 to 2047
- coarse_centroids: float32 [2048, 768], P('cent'), may hold values from -6 to 6
Outputs:
- new_fine: float32 [8192, 768], P('cent')
- new_coarse: float32 [2048, 768], P('cent')
All inputs are finite; a program needn't handle non-finite values.
Results may differ from a plain program's by a relative error of at most 0.004.
Values may be sent and summed in bfloat16 or wider, within the bound.
A program may use at most 64 MiB of HBM per device.

v0:
```python
import math

import jax
import jax.numpy as jnp
from jax import lax
from jax.sharding import PartitionSpec as P

KC = 2048


sharpness = 0.1
coarse_prior = 16.0


def block_logits(one_block, narrow_centroids, half_norm):
    scores = lax.dot_general(
        one_block, narrow_centroids, (((1,), (1,)), ((), ())), preferred_element_type=jnp.float32
    )
    return sharpness * (scores - half_norm[None, :])


def coarse_terms(parent_ids, pooled, mass_rows):
    summed = jax.ops.segment_sum(pooled, parent_ids, num_segments=KC)
    weighted = jax.ops.segment_sum(mass_rows, parent_ids, num_segments=KC)
    return (summed, weighted)


def local(embeddings, fine_centroids, parents, coarse_centroids):
    gathered = lax.all_gather(embeddings, "cent", axis=0, tiled=True)
    row_count = gathered.shape[0]
    feat_width = gathered.shape[1]
    block_rows = math.gcd(row_count, 512)
    row_blocks = gathered.reshape(row_count // block_rows, block_rows, feat_width)
    narrow_centroids = fine_centroids.astype(jnp.bfloat16)
    half_norm = 0.5 * jnp.sum(fine_centroids * fine_centroids, axis=1)
    no_carry = jnp.zeros((), jnp.float32)

    def peak_step(carried, one_block):
        logits = block_logits(one_block, narrow_centroids, half_norm)
        return (carried, jnp.max(logits, axis=1))

    _, local_peak = lax.scan(peak_step, no_carry, row_blocks)
    row_peak = lax.pmax(local_peak.reshape(-1), "cent")

    def mass_step(carried, items):
        one_block, block_peak = items
        logits = block_logits(one_block, narrow_centroids, half_norm)
        return (carried, jnp.sum(jnp.exp(logits - block_peak[:, None]), axis=1))

    _, local_mass = lax.scan(mass_step, no_carry, (row_blocks, row_peak.reshape(-1, block_rows)))
    row_mass = lax.psum(local_mass.reshape(-1), "cent")

    def sum_step(carried, items):
        one_block, block_peak, block_mass = items
        logits = block_logits(one_block, narrow_centroids, half_norm)
        soft_weights = jnp.exp(logits - block_peak[:, None]) / block_mass[:, None]
        wide_block = one_block.astype(jnp.float32)
        summed = carried[0] + lax.dot_general(
            soft_weights,
            wide_block,
            (((0,), (0,)), ((), ())),
            precision=lax.Precision.HIGHEST,
            preferred_element_type=jnp.float32,
        )
        counted = carried[1] + jnp.sum(soft_weights, axis=0)
        return ((summed, counted), None)

    local_rows = fine_centroids.shape[0]
    start_state = (
        jnp.zeros(fine_centroids.shape, jnp.float32),
        jnp.zeros((local_rows,), jnp.float32),
    )
    stacked = (row_blocks, row_peak.reshape(-1, block_rows), row_mass.reshape(-1, block_rows))
    (fine_sums, fine_counts), _ = lax.scan(sum_step, start_state, stacked)
    total_sums, total_counts = lax.psum((fine_sums, fine_counts), "dp")
    pooled = fine_centroids + total_sums
    mass_rows = 1.0 + total_counts
    new_fine = pooled / mass_rows[:, None]
    col_width = feat_width // lax.axis_size("dp")
    first_col = lax.axis_index("dp") * col_width
    pooled_cols = lax.dynamic_slice_in_dim(pooled, first_col, col_width, 1)
    coarse_sum, coarse_mass = coarse_terms(parents, pooled_cols, mass_rows)
    owned_sum, owned_mass = (
        lax.psum_scatter(coarse_sum, "cent", scatter_dimension=0, tiled=True),
        lax.psum_scatter(coarse_mass, "cent", scatter_dimension=0, tiled=True),
    )
    old_cols = lax.dynamic_slice_in_dim(coarse_centroids, first_col, col_width, 1)
    new_cols = (coarse_prior * old_cols + owned_sum) / (coarse_prior + owned_mass)[:, None]
    new_coarse = lax.all_gather(new_cols, "dp", axis=1, tiled=True)
    return (new_fine, new_coarse)


def solution(mesh):
    in_specs = (P(("dp", "cent"), None), P("cent", None), P("cent"), P("cent", None))
    out_specs = (P("cent", None), P("cent", None))
    return jax.shard_map(local, mesh=mesh, in_specs=in_specs, out_specs=out_specs, check_vma=False)
```

profile of v0, /device:TPU:0, one launch (start us, length us, event | category | flops | bytes accessed | tf_op | source)
XLA Modules:
  0.0 365.5 jit_solution(11755867619514082077)
XLA Ops:
  7.2 0.0 all-gather.2.cloned.1.call-start
  7.2 0.7 all-gather.2.cloned.1.call-update
  7.9 0.0 all-reduce.3.cloned.1.call-start
  8.0 2.1 multiply_reduce_fusion
  10.1 71.3 %all-gather.2.cloned.1.call-done = bf16[2048,768]{1,0:T(8,128)(2,1)} async-done(((bf16[128,768]{1,0:T(8,128)(2,1)}), bf16[2048,768]{1,0:T(8,128)(2,1)}) %all-gather.2.cloned.1.call-update) | async-done | bytes 3145744 | tf_op jit(solution)/shard_map/all_gather | solution.py:29
  81.4 7.3 %while.33 = (s32[]{:T(128)}, f32[4,512]{1,0:T(4,128)S(1)}, bf16[4,512,768]{2,1,0:T(8,128)(2,1)}, bf16[512,768]{1,0:T(8,128)(2,1)S(1)}, f32[512]{0:T(512)S(1)}, /*index=5*/s32[]{:T(128)}, s32[]{:T(128)}) while((s32[]{:T(128)}, f32[4,512]{1,0:T(4,128)S(1)}, bf16[4,512,768]{2,1,0:T(8,128)(2,1)}, bf16[512,768]{1,0:T(8,128)(2,1)S(1)}, ...), condition=%wide.region_3.4_spmd, body=%wide.region_1.3_spmd.sunk | while | flops 403439104 | bytes 1581649 | solution.py:42
  81.4 1.7 fusion.44
  83.1 0.1 dynamic_update_slice.9
  83.2 1.8 fusion.44
  85.0 0.1 dynamic_update_slice.9
  85.0 1.8 fusion.44
  86.8 0.1 dynamic_update_slice.9
  86.8 1.8 fusion.44
  88.6 0.1 dynamic_update_slice.9
  88.7 39.8 %pmax.7 = f32[4,512]{1,0:T(4,128)S(1)} all-reduce(f32[4,512]{1,0:T(4,128)S(1)} %get-tuple-element.104), channel_id=1, replica_groups=mesh['dp'=2,'cent'=16] {'cent'}, use_global_device_ids=true, to_apply=%region_4.5 | all-reduce | flops 2048 | bytes 16384 | tf_op jit(solution)/shard_map/pmax | solution.py:43
  128.5 7.7 %while.34 = (s32[]{:T(128)}, f32[4,512]{1,0:T(4,128)S(1)}, bf16[4,512,768]{2,1,0:T(8,128)(2,1)}, bf16[512,768]{1,0:T(8,128)(2,1)S(1)}, f32[512]{0:T(512)S(1)}, /*index=5*/f32[4,512]{1,0:T(4,128)S(1)}, s32[]{:T(128)}, s32[]{:T(128)}) while((s32[]{:T(128)}, f32[4,512]{1,0:T(4,128)S(1)}, bf16[4,512,768]{2,1,0:T(8,128)(2,1)}, ...), condition=%wide.region_7.8_spmd, body=%wide.region_5.7_spmd.sunk | while | flops 403701248 | bytes 1587805 | solution.py:50
  128.5 1.8 fusion.47
  130.4 0.1 dynamic_update_slice.10
  130.5 1.8 fusion.47
  132.3 0.1 dynamic_update_slice.10
  132.4 1.8 fusion.47
  134.2 0.1 dynamic_update_slice.10
  134.3 1.8 fusion.47
  136.1 0.1 dynamic_update_slice.10
  136.2 37.1 %psum.21 = f32[4,512]{1,0:T(4,128)S(1)} all-reduce(f32[4,512]{1,0:T(4,128)S(1)} %get-tuple-element.105), channel_id=1, replica_groups=mesh['dp'=2,'cent'=16] {'cent'}, use_global_device_ids=true, to_apply=%region_8.9 | all-reduce | flops 2048 | bytes 16384 | tf_op jit(solution)/shard_map/psum | solution.py:51
  173.3 20.2 %while.35 = (s32[]{:T(128)}, f32[512,768]{1,0:T(8,128)S(1)}, f32[512]{0:T(512)S(1)}, bf16[4,512,768]{2,1,0:T(8,128)(2,1)}, bf16[512,768]{1,0:T(8,128)(2,1)S(1)},...) while((s32[]{:T(128)}, f32[512,768]{1,0:T(8,128)S(1)}, ...), condition=%wide.region_11.12_spmd.clone, body=%wide.region_9.11_spmd.clone.sunk | while | flops 2820669952 | bytes 7625844 | solution.py:74
  173.4 1.9 fusion.51
  175.2 3.1 select_add_fusion.4
  178.4 1.9 fusion.51
  180.3 3.1 select_add_fusion.4
  183.5 1.9 fusion.51
  185.4 3.1 select_add_fusion.4
  188.6 1.9 fusion.51
  190.4 3.1 select_add_fusion.4
  193.6 0.0 copy-start
  193.6 0.0 copy-start.1
  193.6 1.1 copy-done
  194.7 0.0 all-reduce.3.cloned.1.call-update
  194.8 0.0 reduce-scatter.2.cloned.1.call-start
  194.8 2.5 psum.23
  197.3 15.7 %all-reduce.3.cloned.1.call-done = f32[512,768]{1,0:T(8,128)} async-done(((f32[512,768]{1,0:T(8,128)}), f32[512,768]{1,0:T(8,128)}) %all-reduce.3.cloned.1.call-update) | async-done | bytes 1572880 | tf_op jit(solution)/shard_map/psum | solution.py:75
  213.0 0.0 copy-done.1
  213.0 2.8 broadcast_divide_fusion
  215.8 5.6 %scatter_custom_fusion = f32[2048,384]{1,0:T(8,128)} fusion(s32[512]{0:T(512)} %param.12, f32[]{:T(128)} %constant.35.clone.1, f32[512,768]{1,0:T(8,128)S(1)} %get-tuple-element.174, s32[]{:T(128)} %constant.39.clone.1, s32[]{:T(128)S(6)} %select_n.4), kind=kCustom, calls=%fused_computation.32 | custom fusion | flops 196608 | bytes 3933188 | tf_op jit(solution)/shard_map/scatter-add | solution.py:23
  221.4 0.0 copy-start.3
  221.4 0.0 copy-start.2
  221.4 0.0 reduce-scatter.2.cloned.1.call-update
  221.4 0.6 copy-done.3
  222.0 0.6 dynamic-slice
  223.3 3.4 scatter_custom_fusion.1
  226.7 42.8 %all-reduce = f32[2048]{0:T(1024)S(1)} all-reduce(f32[2048]{0:T(1024)S(1)} %scatter_custom_fusion.1), channel_id=3, replica_groups=mesh['dp'=2,'cent'=16] {'cent'}, use_global_device_ids=true, to_apply=%region_17.18.clone | all-reduce | flops 2048 | bytes 16384
  269.5 0.1 dynamic-slice_add_fusion
  269.5 85.6 %reduce-scatter.2.cloned.1.call-done = f32[128,384]{1,0:T(8,128)} async-done(((f32[2048,384]{1,0:T(8,128)}), f32[128,384]{1,0:T(8,128)}) %reduce-scatter.2.cloned.1.call-update) | async-done | bytes 196624 | tf_op jit(solution)/shard_map/reduce_scatter | solution.py:84
  355.1 0.0 copy-done.2
  355.1 1.0 add_divide_fusion
  356.2 2.1 all_gather.7
  358.2 0.7 copy.33
  (18 shorter events, 0.1 us)
Async XLA Ops:
  7.2 74.2 %all-gather.2.cloned.1.call-start = ((), (), s32[]{:S(2)}) async-start(), calls=%async_computation.1 | async-start | bytes 3342336 | tf_op jit(solution)/shard_map/all_gather | solution.py:29
  7.9 205.1 %all-reduce.3.cloned.1.call-start = ((), (), s32[]{:S(2)}) async-start(), calls=%async_computation.2 | async-start | bytes 3145728 | tf_op jit(solution)/shard_map/psum | solution.py:75
  193.6 1.1 copy-start
  193.6 19.4 %copy-start.1 = (f32[512,768]{1,0:T(8,128)S(1)}, f32[512,768]{1,0:T(8,128)}, u32[]{:S(2)}) copy-start(f32[512,768]{1,0:T(8,128)} %param.11) | copy-start | bytes 4718596
  194.8 160.4 %reduce-scatter.2.cloned.1.call-start = ((), (), s32[]{:S(2)}) async-start(), calls=%async_computation.3 | async-start | bytes 3342336 | tf_op jit(solution)/shard_map/reduce_scatter | solution.py:84
  221.4 0.7 copy-start.3
  221.4 133.8 %copy-start.2 = (f32[128,768]{1,0:T(8,128)S(1)}, f32[128,768]{1,0:T(8,128)}, u32[]{:S(2)}) copy-start(f32[128,768]{1,0:T(8,128)} %param.13) | copy-start | bytes 1179652
Sparse Core Ops, SparseCore 0:
  10.7 70.5 all-gather.1
  194.9 18.0 all-reduce.2
  221.5 133.5 reduce-scatter.1
where the time goes:
time: 367 us; the launch traced here: 366 us
  waiting for transfers between devices  173 us (47%)
  blocking collectives  124 us (34%)
  matrix products  34.3 us (9%)
  other arithmetic  15.1 us (4%)
  between operations  14.5 us (4%)
    reduce_scatter x1, waiting for transfers between devices, local(): lax.psum_scatter(coarse_sum, 'cent', scatter_dimension=0, tiled=True)  85.6 us
    all_gather x1, waiting for transfers between devices, local(): gathered = lax.all_gather(embeddings, 'cent', axis=0, tiled=True)  71.3 us
    unnamed x1, blocking collectives  42.8 us
    pmax x1, blocking collectives, local(): row_peak = lax.pmax(local_peak.reshape(-1), 'cent')  39.8 us
    psum x1, blocking collectives, local(): row_mass = lax.psum(local_mass.reshape(-1), 'cent')  37.1 us
    dot_general x12, matrix products, block_logits(): lax.dot_general(one_block, narrow_centroids, (((1,), (1,)), ((), ())), pr...  21.8 us
    psum x1, waiting for transfers between devices, local(): total_sums, total_counts = lax.psum((fine_sums, fine_counts), 'dp')  15.7 us
    dot_general x4, matrix products, sum_step(): lax.dot_general(soft_weights, wide_block, (((0,), (0,)), ((), ())), preci...  12.5 us
  transfers between devices with their start and end apart: 3, of which 3 were waited for; matrix products, arithmetic and copies ran while one was open for 2% of the time, Pallas kernels for 0%

commit v1 on v0

--- a/solution.py
+++ b/solution.py
@@ -1,8 +1,11 @@
+import functools
 import math
 
 import jax
 import jax.numpy as jnp
 from jax import lax
+from jax.experimental import pallas as pl
+from jax.experimental.pallas import tpu as pltpu
 from jax.sharding import PartitionSpec as P
 
 KC = 2048
@@ -90,7 +93,361 @@
     return (new_fine, new_coarse)
 
 
+MESH = pl.DeviceIdType.MESH
+NT = (((1,), (1,)), ((), ()))
+
+
+def dot(a, b):
+    return jnp.dot(a, b, preferred_element_type=jnp.float32)
+
+
+def to_row(col):
+    return jnp.transpose(jnp.broadcast_to(col, (col.shape[0], 128)))[0:8]
+
+
+def to_col(row):
+    return jnp.transpose(jnp.broadcast_to(row, (128, row.shape[1])))[:, 0:1]
+
+
+def step_kernel(
+    n, nz, emb, fine, par, coarse, nf, nc,
+    G, narrow, pr, wh, wl, st, ss, sr, cs, cr, hi, lo,
+    xs, xr, ys, yr, zs, zr, own, ms, mr,
+    g_recv, gz_send, gx_send, gy_send, st_send, st_recv,
+    sum_send, sum_recv, cnt_sem, nf_send, nf_recv,
+    x_send, x_recv, y_send, y_recv, z_send, z_recv, m_sem, nc_sem,
+):
+    d = lax.axis_index("dp")
+    c = lax.axis_index("cent")
+    rows = emb.shape[0]
+    local, width = fine.shape
+    half = width // 2
+    coarse_rows = coarse.shape[0]
+    x, y, z = c % 2, (c // 2) % 2, c // 4
+    xy = c % 4
+    nbr_x = c + 1 - 2 * x
+    nbr_y = c + 2 - 4 * y
+    cols = (xy, xy + 1 - 2 * x, xy + 2 - 4 * y, 3 - xy)
+    other = 1 - d
+
+    barrier = pltpu.get_barrier_semaphore()
+    for k in range(1, n):
+        pl.semaphore_signal(barrier, inc=1, device_id=(d, (c + k) % n), device_id_type=MESH)
+    pl.semaphore_signal(barrier, inc=1, device_id=(other, c), device_id_type=MESH)
+    pl.semaphore_wait(barrier, n)
+
+    def copy(src, dst, send, recv, core, chip):
+        return pltpu.make_async_remote_copy(
+            src_ref=src, dst_ref=dst, send_sem=send, recv_sem=recv,
+            device_id=(core, chip), device_id_type=MESH,
+        )
+
+    def block_copy(src, slot, send, chip):
+        return copy(src, G.at[slot], send, g_recv.at[slot], d, chip)
+
+    def arrived(slot):
+        copy(G.at[slot], G.at[slot], gz_send.at[0], g_recv.at[slot], d, nbr_x).wait_recv()
+
+    mine = xy * nz + z
+    sends = []
+
+    def send_block(src, slot, send, chip):
+        one = block_copy(src, slot, send, chip)
+        one.start()
+        sends.append(one)
+
+    send_block(emb, mine, gx_send.at[0], nbr_x)
+    send_block(emb, mine, gy_send.at[0], nbr_y)
+    for k in range(1, nz):
+        send_block(emb, mine, gz_send.at[k - 1], ((z + k) % nz) * 4 + xy)
+    G[mine] = emb[...]
+    narrow[...] = fine[...].astype(jnp.bfloat16)
+    half_norm = 0.5 * jnp.sum(fine[...] * fine[...], axis=1, keepdims=True)
+
+    def group_logits(r):
+        col = cols[r]
+
+        def pair(i, _):
+            blocks = G[pl.ds(col * nz + 2 * i, 2)].reshape(2 * rows, width)
+            scores = lax.dot_general(narrow[...], blocks, NT, preferred_element_type=jnp.float32)
+            logits = sharpness * (scores - half_norm)
+            peak = jnp.max(logits, axis=0, keepdims=True)
+            weights = jnp.exp(logits - peak)
+            mass = jnp.sum(weights, axis=0, keepdims=True)
+            pr[r, :, pl.ds(pl.multiple_of(i * (2 * rows), 2 * rows), 2 * rows)] = weights
+            for t in range(2):
+                st[col, 0, pl.ds(2 * i + t, 1), :] = peak[:, t * rows:(t + 1) * rows]
+                st[col, 0, pl.ds(nz + 2 * i + t, 1), :] = mass[:, t * rows:(t + 1) * rows]
+            return 0
+
+        lax.fori_loop(0, nz // 2, pair, 0)
+
+    def send_stats(r):
+        col = cols[r]
+        for k in range(1, n):
+            copy(
+                st.at[col, 0], st.at[col, n - k], st_send.at[r], st_recv.at[col], d, (c + k) % n
+            ).start()
+
+    for k in range(1, nz):
+        slot = xy * nz + (z + nz - k) % nz
+        arrived(slot)
+        send_block(G.at[slot], slot, gx_send.at[k], nbr_x)
+        send_block(G.at[slot], slot, gy_send.at[k], nbr_y)
+    for k in range(nz // 2):
+        slot = cols[1] * nz + (z + nz - k) % nz
+        arrived(slot)
+        send_block(G.at[slot], slot, gy_send.at[nz + k], nbr_y)
+    for k in range(nz // 2, nz):
+        slot = cols[2] * nz + (z + nz - k) % nz
+        arrived(slot)
+        send_block(G.at[slot], slot, gx_send.at[nz + k - nz // 2], nbr_x)
+    group_logits(0)
+    send_stats(0)
+    for k in range(nz // 2, nz):
+        arrived(cols[1] * nz + (z + nz - k) % nz)
+    group_logits(1)
+    send_stats(1)
+    for k in range(nz // 2):
+        arrived(cols[2] * nz + (z + nz - k) % nz)
+    group_logits(2)
+    send_stats(2)
+    for k in range(nz):
+        arrived(cols[3] * nz + (z + nz - k) % nz)
+    group_logits(3)
+    send_stats(3)
+
+    counts = jnp.zeros((local, 1), jnp.float32)
+    for r in range(4):
+        col = cols[r]
+        pltpu.make_async_copy(
+            st.at[col, pl.ds(1, n - 1)], st.at[col, pl.ds(1, n - 1)], st_recv.at[col]
+        ).wait()
+        peaks = st[col, :, 0:nz, :]
+        masses = st[col, :, nz:2 * nz, :]
+        top = jnp.max(peaks, axis=0)
+        total = jnp.sum(masses * jnp.exp(peaks - top[None]), axis=0)
+        factor = jnp.exp(peaks[0] - top) / total
+        for t in range(nz):
+            lanes = slice(t * rows, (t + 1) * rows)
+            soft = pr[r, :, lanes] * factor[t:t + 1, :]
+            counts = counts + jnp.sum(soft, axis=1, keepdims=True)
+            high = soft.astype(jnp.bfloat16)
+            wh[r, :, lanes] = high
+            wl[r, :, lanes] = (soft - high.astype(jnp.float32)).astype(jnp.bfloat16)
+    cs[...] = to_row(counts)
+    count_copy = copy(cs, cr, cnt_sem.at[0], cnt_sem.at[1], other, c)
+    count_copy.start()
+
+    own_cols = pl.ds(pl.multiple_of(d * half, 128), half)
+    other_cols = pl.ds(pl.multiple_of(other * half, 128), half)
+    part = local // 2
+
+    def sums(h, columns):
+        picked = pl.ds(h * part, part)
+        out = jnp.zeros((part, half), jnp.float32)
+        for r in range(4):
+            block = G[pl.ds(cols[r] * nz, nz), :, columns].reshape(nz * rows, half)
+            out = out + dot(wh[r, picked, :], block) + dot(wl[r, picked, :], block)
+        return out
+
+    sum_copies = []
+    for h in range(2):
+        ss[h] = sums(h, other_cols)
+        one = copy(ss.at[h], sr.at[h], sum_send.at[h], sum_recv.at[h], other, c)
+        one.start()
+        sum_copies.append(one)
+    own_sums = [sums(h, own_cols) for h in range(2)]
+
+    count_copy.wait()
+    mass_row = 1.0 + (cs[...] + cr[...])
+    mass_col = to_col(mass_row[0:1])
+    nf_copies = []
+    for h in range(2):
+        sum_copies[h].wait()
+        picked = pl.ds(h * part, part)
+        pooled = fine[picked, own_cols] + (own_sums[h] + sr[h])
+        high = pooled.astype(jnp.bfloat16)
+        hi[picked, :] = high
+        lo[picked, :] = (pooled - high.astype(jnp.float32)).astype(jnp.bfloat16)
+        nf[picked, own_cols] = pooled / mass_col[h * part:(h + 1) * part]
+        one = copy(
+            nf.at[picked, own_cols], nf.at[picked, own_cols], nf_send.at[h], nf_recv.at[h], other, c
+        )
+        one.start()
+        nf_copies.append(one)
+
+    one_row = mass_row[0:1]
+    first = one_row.astype(jnp.bfloat16).astype(jnp.float32)
+    second = (one_row - first).astype(jnp.bfloat16).astype(jnp.float32)
+    third = one_row - first - second
+    at_row = lax.broadcasted_iota(jnp.int32, (16, local), 0)
+    pieces = jnp.where(
+        at_row == 0, first, jnp.where(at_row == 1, second, jnp.where(at_row == 2, third, 0.0))
+    ).astype(jnp.bfloat16)
+    place = lax.broadcasted_iota(jnp.int32, (coarse_rows, local), 0)
+
+    def partial_block(chip):
+        hot = (par[...] == place + chip * coarse_rows).astype(jnp.float32).astype(jnp.bfloat16)
+        masses = lax.dot_general(pieces, hot, NT, preferred_element_type=jnp.float32)
+        ms[chip] = jnp.broadcast_to(jnp.sum(masses, axis=0, keepdims=True), (8, coarse_rows))
+        return dot(hot, hi[...]) + dot(hot, lo[...])
+
+    def column_blocks(r, put):
+        def one(t, _):
+            put(t, partial_block(t * 4 + cols[r]))
+            return 0
+
+        lax.fori_loop(0, nz, one, 0)
+
+    low = nz // 2
+
+    def x_copy(i):
+        return copy(xs.at[i], xr.at[i], x_send.at[i], x_recv.at[i], d, nbr_x)
+
+    def y_copy(i):
+        return copy(ys.at[i], yr.at[i], y_send.at[i], y_recv.at[i], d, nbr_y)
+
+    def put_diag(t, value):
+        own[t] = value
+
+    column_blocks(3, put_diag)
+    for t in range(low):
+        xs[nz + t] = own[t].astype(jnp.bfloat16)
+        x_copy(nz + t).start()
+        ys[nz + t] = own[low + t].astype(jnp.bfloat16)
+        y_copy(nz + t).start()
+    column_blocks(1, put_diag)
+    for t in range(low):
+        xs[t] = own[t].astype(jnp.bfloat16)
+        x_copy(t).start()
+    for t in range(low):
+        y_copy(nz + t).wait_recv()
+        xs[low + t] = (own[low + t] + yr[nz + t].astype(jnp.float32)).astype(jnp.bfloat16)
+        x_copy(low + t).start()
+    column_blocks(2, put_diag)
+    for t in range(low):
+        ys[low + t] = own[low + t].astype(jnp.bfloat16)
+        y_copy(low + t).start()
+    for t in range(low):
+        x_copy(nz + t).wait_recv()
+        ys[t] = (own[t] + xr[nz + t].astype(jnp.float32)).astype(jnp.bfloat16)
+        y_copy(t).start()
+    column_blocks(0, put_diag)
+    for k in range(1, n):
+        to = (c + k) % n
+        copy(ms.at[to], mr.at[n - k], m_sem.at[0], m_sem.at[1], d, to).start()
+
+    def column_sum(t):
+        x_copy(t).wait_recv()
+        y_copy(t).wait_recv()
+        return own[t] + (xr[t].astype(jnp.float32) + yr[t].astype(jnp.float32))
+
+    z_copies = []
+    for k in range(1, nz):
+        t = (z + k) % nz
+        zs[k - 1] = column_sum(t).astype(jnp.bfloat16)
+        one = copy(
+            zs.at[k - 1], zr.at[k - 1], z_send.at[k - 1], z_recv.at[k - 1], d, t * 4 + xy
+        )
+        one.start()
+        z_copies.append(one)
+    total = column_sum(z)
+    pltpu.make_async_copy(mr.at[pl.ds(1, n - 1)], mr.at[pl.ds(1, n - 1)], m_sem.at[1]).wait()
+    mass_total = ms[c]
+    for k in range(1, n):
+        mass_total = mass_total + mr[k]
+    mass_total = to_col(mass_total[0:1])
+    for k in range(1, nz):
+        z_copies[k - 1].wait_recv()
+        total = total + zr[k - 1].astype(jnp.float32)
+    nc[:, own_cols] = (coarse_prior * coarse[:, own_cols] + total) / (coarse_prior + mass_total)
+    last = copy(nc.at[:, own_cols], nc.at[:, own_cols], nc_sem.at[0], nc_sem.at[1], other, c)
+    last.start()
+
+    for one in sends + z_copies:
+        one.wait_send()
+    for r in range(4):
+        whole = st.at[cols[r], pl.ds(1, n - 1)]
+        pltpu.make_async_copy(whole, whole, st_send.at[r]).wait()
+    pltpu.make_async_copy(mr.at[pl.ds(1, n - 1)], mr.at[pl.ds(1, n - 1)], m_sem.at[0]).wait()
+    for i in range(nz + low):
+        x_copy(i).wait_send()
+        y_copy(i).wait_send()
+    for one in nf_copies:
+        one.wait()
+    last.wait()
+
+
+def fused_step(n, embeddings, fine_centroids, parents, coarse_centroids):
+    nz = n // 4
+    low = nz // 2
+    rows, width = embeddings.shape
+    local = fine_centroids.shape[0]
+    coarse_rows = coarse_centroids.shape[0]
+    half = width // 2
+    bf, f32 = jnp.bfloat16, jnp.float32
+    vmem = pl.BlockSpec(memory_space=pltpu.VMEM)
+    dma = pltpu.SemaphoreType.DMA
+    V = pltpu.VMEM
+    block = (coarse_rows, half)
+    return pl.pallas_call(
+        functools.partial(step_kernel, n, nz),
+        out_shape=(
+            jax.ShapeDtypeStruct(fine_centroids.shape, f32),
+            jax.ShapeDtypeStruct(coarse_centroids.shape, f32),
+        ),
+        in_specs=[vmem] * 4,
+        out_specs=(vmem, vmem),
+        scratch_shapes=[
+            V((n, rows, width), bf),
+            V((local, width), bf),
+            V((4, local, nz * rows), f32),
+            V((4, local, nz * rows), bf),
+            V((4, local, nz * rows), bf),
+            V((4, n, 2 * nz, rows), f32),
+            V((2, local // 2, half), f32),
+            V((2, local // 2, half), f32),
+            V((8, local), f32),
+            V((8, local), f32),
+            V((local, half), bf),
+            V((local, half), bf),
+            V((nz + low,) + block, bf),
+            V((nz + low,) + block, bf),
+            V((nz + low,) + block, bf),
+            V((nz + low,) + block, bf),
+            V((nz - 1,) + block, bf),
+            V((nz - 1,) + block, bf),
+            V((nz,) + block, f32),
+            V((n, 8, coarse_rows), f32),
+            V((n, 8, coarse_rows), f32),
+            dma((n,)), dma((nz - 1,)), dma((nz + low,)), dma((nz + low,)),
+            dma((4,)), dma((4,)),
+            dma((2,)), dma((2,)), dma((2,)), dma((2,)), dma((2,)),
+            dma((nz + low,)), dma((nz + low,)), dma((nz + low,)), dma((nz + low,)),
+            dma((nz - 1,)), dma((nz - 1,)), dma((2,)), dma((2,)),
+        ],
+        compiler_params=pltpu.CompilerParams(collective_id=0, has_side_effects=True),
+    )(embeddings, fine_centroids, parents.reshape(1, local), coarse_centroids)
+
+
 def solution(mesh):
     in_specs = (P(("dp", "cent"), None), P("cent", None), P("cent"), P("cent", None))
     out_specs = (P("cent", None), P("cent", None))
-    return jax.shard_map(local, mesh=mesh, in_specs=in_specs, out_specs=out_specs, check_vma=False)
+    n, cores = mesh.shape["cent"], mesh.shape["dp"]
+
+    def body(embeddings, fine_centroids, parents, coarse_centroids):
+        rows, width = embeddings.shape
+        fits = (
+            cores == 2
+            and n % 8 == 0
+            and rows == 128
+            and width % 256 == 0
+            and fine_centroids.shape[0] % 256 == 0
+            and coarse_centroids.shape[0] == 128
+        )
+        if fits:
+            return fused_step(n, embeddings, fine_centroids, parents, coarse_centroids)
+        return local(embeddings, fine_centroids, parents, coarse_centroids)
+
+    return jax.shard_map(body, mesh=mesh, in_specs=in_specs, out_specs=out_specs, check_vma=False)

time: 367 us -> 88.8 us (0.24)
  waiting for transfers between devices: 173 us -> 0 us
  blocking collectives: 124 us -> 0 us
  Pallas kernels: 0 us -> 84.5 us
  matrix products: 34.3 us -> 0 us
  other arithmetic: 15.1 us -> 0 us
  between operations: 14.5 us -> 0.65 us
    reduce_scatter x1 -> x0, waiting for transfers between devices: 85.6 us -> none  [local(): lax.psum_scatter(coarse_sum, 'cent', scatter_dimension=0, tiled=True)]
    pallas_call x0 -> x1, Pallas kernels: none -> 84.5 us  [fused_step(): pl.pallas_call(functools.partial(step_kernel, n, nz), out_shape=(jax.Shap...]
    all_gather x1 -> x0, waiting for transfers between devices: 71.3 us -> none  [local(): gathered = lax.all_gather(embeddings, 'cent', axis=0, tiled=True)]
    unnamed x1 -> x0, blocking collectives: 42.8 us -> none
    pmax x1 -> x0, blocking collectives: 39.8 us -> none  [local(): row_peak = lax.pmax(local_peak.reshape(-1), 'cent')]
    psum x2 -> x0, blocking collectives: 39.6 us -> none  [the longest x1 37.1 us: local(): row_mass = lax.psum(local_mass.reshape(-1), 'cent')]
    dot_general x16 -> x0, matrix products: 34.3 us -> none  [the longest x12 21.8 us: block_logits(): lax.dot_general(one_block, narrow_centroids, (((1,), (1,)), ((), ())), pr...]
    psum x1 -> x0, waiting for transfers between devices: 15.7 us -> none  [local(): total_sums, total_counts = lax.psum((fine_sums, fine_counts), 'dp')]
  transfers between devices with their start and end apart: 3 -> 0, of which waited for: 3 -> 0; matrix products, arithmetic and copies ran while one was open for 2% -> 0% of each run, Pallas kernels for 0% -> 0%
where the time goes in v1:
time: 88.8 us; the launch traced here: 88.6 us
  Pallas kernels  84.5 us (95%)
  local copies, waits for them, and re-layouts  3.45 us (4%)
    pallas_call x1, Pallas kernels, fused_step(): pl.pallas_call(functools.partial(step_kernel, n, nz), out_shape=(jax.Shap...  84.5 us
    unnamed x4, local copies, waits for them, and re-layouts  3.45 us

profile of v1, /device:TPU:0, one launch (start us, length us, event | category | flops | bytes accessed | tf_op | source)
XLA Modules:
  0.0 88.6 jit_solution(532447560906864460)
XLA Ops:
  0.6 84.5 %shard_map.59 = (f32[512,768]{1,0:T(8,128)}, f32[128,768]{1,0:T(8,128)}) custom-call(bf16[128,768]{1,0:T(8,128)(2,1)} %emb.1, f32[512,768]{1,0:T(8,128)} %fine.1, s32[1,512]{1,0:T(1,128)} %bitcast.1, f32[128,768]{1,0:T(8,128)} %coarse.1), custom_call_target="tpu_custom_call" | custom-call | tf_op jit(solution)/shard_map/pallas_call | solution.py:394
  85.1 0.0 copy-start
  85.1 2.7 %copy.8 = f32[512,768]{1,0:T(8,128)} copy(f32[512,768]{1,0:T(8,128)} %get-tuple-element.4) | data formatting | bytes 3145728
  87.8 0.0 copy-done
  87.8 0.7 copy.9
Async XLA Ops:
  85.1 2.7 %copy-start = (f32[128,768]{1,0:T(8,128)S(1)}, f32[128,768]{1,0:T(8,128)}, u32[]{:S(2)}) copy-start(f32[128,768]{1,0:T(8,128)} %get-tuple-element.5) | copy-start | bytes 1179652

commit v2 on v1

--- a/solution.py
+++ b/solution.py
@@ -142,45 +142,67 @@
             device_id=(core, chip), device_id_type=MESH,
         )
 
-    def block_copy(src, slot, send, chip):
-        return copy(src, G.at[slot], send, g_recv.at[slot], d, chip)
-
-    def arrived(slot):
-        copy(G.at[slot], G.at[slot], gz_send.at[0], g_recv.at[slot], d, nbr_x).wait_recv()
-
-    mine = xy * nz + z
+    def near(i):
+        mirror = z >= nz // 2
+        at = jnp.where(mirror, nz - 1 - z, z)
+        step = (i + 1) // 2
+        found = jnp.where(i <= 2 * at, at - step if i % 2 else at + step, i)
+        return jnp.where(mirror, nz - 1 - found, found)
+
+    order = [near(i) for i in range(nz)]
+    low = nz // 2
+
+    piece = rows // 2
+
+    def piece_of(slot, h):
+        return G.at[slot, pl.ds(h * piece, piece)]
+
+    def piece_copy(src, slot, h, send, chip):
+        return copy(src, piece_of(slot, h), send, g_recv.at[slot * 2 + h], d, chip)
+
+    def arrived(slot, h):
+        piece_copy(piece_of(slot, h), slot, h, gx_send.at[0], nbr_x).wait_recv()
+
     sends = []
-
-    def send_block(src, slot, send, chip):
-        one = block_copy(src, slot, send, chip)
+    maybe_sends = []
+
+    def send_piece(src, slot, h, send, chip):
+        one = piece_copy(src, slot, h, send, chip)
         one.start()
         sends.append(one)
 
-    send_block(emb, mine, gx_send.at[0], nbr_x)
-    send_block(emb, mine, gy_send.at[0], nbr_y)
-    for k in range(1, nz):
-        send_block(emb, mine, gz_send.at[k - 1], ((z + k) % nz) * 4 + xy)
+    def send_along(src, slot, h, send, to_z):
+        exists = jnp.logical_and(to_z >= 0, to_z < nz)
+        one = piece_copy(src, slot, h, send, to_z * 4 + xy)
+
+        @pl.when(exists)
+        def _():
+            one.start()
+
+        maybe_sends.append((exists, one))
+
+    mine = xy * nz + z
+    for h in range(2):
+        src = emb.at[pl.ds(h * piece, piece)]
+        send_along(src, mine, h, gz_send.at[h], z + 1)
+        send_along(src, mine, h, gz_send.at[2 + h], z - 1)
+        send_piece(src, mine, h, gx_send.at[h], nbr_x)
+        send_piece(src, mine, h, gy_send.at[h], nbr_y)
     G[mine] = emb[...]
     narrow[...] = fine[...].astype(jnp.bfloat16)
     half_norm = 0.5 * jnp.sum(fine[...] * fine[...], axis=1, keepdims=True)
 
-    def group_logits(r):
-        col = cols[r]
-
-        def pair(i, _):
-            blocks = G[pl.ds(col * nz + 2 * i, 2)].reshape(2 * rows, width)
-            scores = lax.dot_general(narrow[...], blocks, NT, preferred_element_type=jnp.float32)
-            logits = sharpness * (scores - half_norm)
-            peak = jnp.max(logits, axis=0, keepdims=True)
-            weights = jnp.exp(logits - peak)
-            mass = jnp.sum(weights, axis=0, keepdims=True)
-            pr[r, :, pl.ds(pl.multiple_of(i * (2 * rows), 2 * rows), 2 * rows)] = weights
-            for t in range(2):
-                st[col, 0, pl.ds(2 * i + t, 1), :] = peak[:, t * rows:(t + 1) * rows]
-                st[col, 0, pl.ds(nz + 2 * i + t, 1), :] = mass[:, t * rows:(t + 1) * rows]
-            return 0
-
-        lax.fori_loop(0, nz // 2, pair, 0)
+    def block_logits(r, i):
+        col, o = cols[r], order[i]
+        scores = lax.dot_general(
+            narrow[...], G[col * nz + o], NT, preferred_element_type=jnp.float32
+        )
+        logits = sharpness * (scores - half_norm)
+        peak = jnp.max(logits, axis=0, keepdims=True)
+        weights = jnp.exp(logits - peak)
+        pr[r, :, pl.ds(pl.multiple_of(o * rows, rows), rows)] = weights
+        st[col, 0, pl.ds(o, 1), :] = peak
+        st[col, 0, pl.ds(nz + o, 1), :] = jnp.sum(weights, axis=0, keepdims=True)
 
     def send_stats(r):
         col = cols[r]
@@ -189,32 +211,45 @@
                 st.at[col, 0], st.at[col, n - k], st_send.at[r], st_recv.at[col], d, (c + k) % n
             ).start()
 
-    for k in range(1, nz):
-        slot = xy * nz + (z + nz - k) % nz
-        arrived(slot)
-        send_block(G.at[slot], slot, gx_send.at[k], nbr_x)
-        send_block(G.at[slot], slot, gy_send.at[k], nbr_y)
-    for k in range(nz // 2):
-        slot = cols[1] * nz + (z + nz - k) % nz
-        arrived(slot)
-        send_block(G.at[slot], slot, gy_send.at[nz + k], nbr_y)
-    for k in range(nz // 2, nz):
-        slot = cols[2] * nz + (z + nz - k) % nz
-        arrived(slot)
-        send_block(G.at[slot], slot, gx_send.at[nz + k - nz // 2], nbr_x)
-    group_logits(0)
+    def forward_column(i):
+        o = order[i]
+        slot = xy * nz + o
+        to_z = jnp.where(o < z, z + 1, z - 1)
+        for h in range(2):
+            arrived(slot, h)
+            block = piece_of(slot, h)
+            send_along(block, slot, h, gz_send.at[2 * i + 2 + h], to_z)
+            send_piece(block, slot, h, gx_send.at[2 * i + h], nbr_x)
+            send_piece(block, slot, h, gy_send.at[2 * i + h], nbr_y)
+
+    def forward_sides(i):
+        o = order[i]
+        for h in range(2):
+            for r in (1, 2):
+                arrived(cols[r] * nz + o, h)
+            if i < low:
+                slot = cols[1] * nz + o
+                send_piece(piece_of(slot, h), slot, h, gy_send.at[2 * (nz + i) + h], nbr_y)
+            else:
+                slot = cols[2] * nz + o
+                send_piece(piece_of(slot, h), slot, h, gx_send.at[2 * (nz + i - low) + h], nbr_x)
+
+    block_logits(0, 0)
+    for i in range(1, nz):
+        forward_column(i)
+        forward_sides(i - 1)
+        block_logits(0, i)
+        block_logits(1, i - 1)
+        block_logits(2, i - 1)
     send_stats(0)
-    for k in range(nz // 2, nz):
-        arrived(cols[1] * nz + (z + nz - k) % nz)
-    group_logits(1)
-    send_stats(1)
-    for k in range(nz // 2):
-        arrived(cols[2] * nz + (z + nz - k) % nz)
-    group_logits(2)
-    send_stats(2)
-    for k in range(nz):
-        arrived(cols[3] * nz + (z + nz - k) % nz)
-    group_logits(3)
+    forward_sides(nz - 1)
+    for r in (1, 2):
+        block_logits(r, nz - 1)
+        send_stats(r)
+    for i in range(nz):
+        for h in range(2):
+            arrived(cols[3] * nz + order[i], h)
+        block_logits(3, i)
     send_stats(3)
 
     counts = jnp.zeros((local, 1), jnp.float32)
@@ -293,80 +328,81 @@
         ms[chip] = jnp.broadcast_to(jnp.sum(masses, axis=0, keepdims=True), (8, coarse_rows))
         return dot(hot, hi[...]) + dot(hot, lo[...])
 
-    def column_blocks(r, put):
-        def one(t, _):
-            put(t, partial_block(t * 4 + cols[r]))
-            return 0
-
-        lax.fori_loop(0, nz, one, 0)
-
-    low = nz // 2
-
     def x_copy(i):
         return copy(xs.at[i], xr.at[i], x_send.at[i], x_recv.at[i], d, nbr_x)
 
     def y_copy(i):
         return copy(ys.at[i], yr.at[i], y_send.at[i], y_recv.at[i], d, nbr_y)
 
-    def put_diag(t, value):
-        own[t] = value
-
-    column_blocks(3, put_diag)
+    def partial(r, i):
+        return partial_block(order[i] * 4 + cols[r])
+
+    def send_x(i, value):
+        xs[i] = value.astype(jnp.bfloat16)
+        x_copy(i).start()
+
+    def send_y(i, value):
+        ys[i] = value.astype(jnp.bfloat16)
+        y_copy(i).start()
+
     for t in range(low):
-        xs[nz + t] = own[t].astype(jnp.bfloat16)
-        x_copy(nz + t).start()
-        ys[nz + t] = own[low + t].astype(jnp.bfloat16)
-        y_copy(nz + t).start()
-    column_blocks(1, put_diag)
+        send_x(nz + t, partial(3, nz - 1 - t))
+        send_y(nz + t, partial(3, low - 1 - t))
     for t in range(low):
-        xs[t] = own[t].astype(jnp.bfloat16)
-        x_copy(t).start()
+        i = nz - 1 - t
+        send_x(i, partial(1, i))
+        far = partial(2, i)
+        x_copy(nz + t).wait_recv()
+        send_y(i, far + xr[nz + t].astype(jnp.float32))
     for t in range(low):
+        i = low - 1 - t
+        send_y(i, partial(2, i))
+        close = partial(1, i)
         y_copy(nz + t).wait_recv()
-        xs[low + t] = (own[low + t] + yr[nz + t].astype(jnp.float32)).astype(jnp.bfloat16)
-        x_copy(low + t).start()
-    column_blocks(2, put_diag)
-    for t in range(low):
-        ys[low + t] = own[low + t].astype(jnp.bfloat16)
-        y_copy(low + t).start()
-    for t in range(low):
-        x_copy(nz + t).wait_recv()
-        ys[t] = (own[t] + xr[nz + t].astype(jnp.float32)).astype(jnp.bfloat16)
-        y_copy(t).start()
-    column_blocks(0, put_diag)
+        send_x(i, close + yr[nz + t].astype(jnp.float32))
+    for i in range(nz):
+        own[i] = partial(0, i)
     for k in range(1, n):
         to = (c + k) % n
         copy(ms.at[to], mr.at[n - k], m_sem.at[0], m_sem.at[1], d, to).start()
 
-    def column_sum(t):
-        x_copy(t).wait_recv()
-        y_copy(t).wait_recv()
-        return own[t] + (xr[t].astype(jnp.float32) + yr[t].astype(jnp.float32))
-
-    z_copies = []
-    for k in range(1, nz):
-        t = (z + k) % nz
-        zs[k - 1] = column_sum(t).astype(jnp.bfloat16)
-        one = copy(
-            zs.at[k - 1], zr.at[k - 1], z_send.at[k - 1], z_recv.at[k - 1], d, t * 4 + xy
-        )
-        one.start()
-        z_copies.append(one)
-    total = column_sum(z)
+    def column_sum(i):
+        x_copy(i).wait_recv()
+        y_copy(i).wait_recv()
+        return own[i] + (xr[i].astype(jnp.float32) + yr[i].astype(jnp.float32))
+
+    def z_copy(i):
+        to_z = order[i]
+        return copy(
+            zs.at[i], zr.at[z], z_send.at[i], z_recv.at[z], d, to_z * 4 + xy
+        )
+
+    for i in range(nz - 1, 0, -1):
+        zs[i] = column_sum(i).astype(jnp.bfloat16)
+        z_copy(i).start()
+    total = column_sum(0)
     pltpu.make_async_copy(mr.at[pl.ds(1, n - 1)], mr.at[pl.ds(1, n - 1)], m_sem.at[1]).wait()
     mass_total = ms[c]
     for k in range(1, n):
         mass_total = mass_total + mr[k]
     mass_total = to_col(mass_total[0:1])
-    for k in range(1, nz):
-        z_copies[k - 1].wait_recv()
-        total = total + zr[k - 1].astype(jnp.float32)
+    for i in range(nz - 1, 0, -1):
+        o = order[i]
+        copy(zs.at[i], zr.at[o], z_send.at[i], z_recv.at[o], d, o * 4 + xy).wait_recv()
+        total = total + zr[o].astype(jnp.float32)
     nc[:, own_cols] = (coarse_prior * coarse[:, own_cols] + total) / (coarse_prior + mass_total)
     last = copy(nc.at[:, own_cols], nc.at[:, own_cols], nc_sem.at[0], nc_sem.at[1], other, c)
     last.start()
 
-    for one in sends + z_copies:
+    for one in sends:
         one.wait_send()
+    for exists, one in maybe_sends:
+        @pl.when(exists)
+        def _(one=one):
+            one.wait_send()
+
+    for i in range(1, nz):
+        z_copy(i).wait_send()
     for r in range(4):
         whole = st.at[cols[r], pl.ds(1, n - 1)]
         pltpu.make_async_copy(whole, whole, st_send.at[r]).wait()
@@ -416,16 +452,16 @@
             V((nz + low,) + block, bf),
             V((nz + low,) + block, bf),
             V((nz + low,) + block, bf),
-            V((nz - 1,) + block, bf),
-            V((nz - 1,) + block, bf),
+            V((nz,) + block, bf),
+            V((nz,) + block, bf),
             V((nz,) + block, f32),
             V((n, 8, coarse_rows), f32),
             V((n, 8, coarse_rows), f32),
-            dma((n,)), dma((nz - 1,)), dma((nz + low,)), dma((nz + low,)),
+            dma((2 * n,)), dma((2 * nz + 2,)), dma((2 * (nz + low),)), dma((2 * (nz + low),)),
             dma((4,)), dma((4,)),
             dma((2,)), dma((2,)), dma((2,)), dma((2,)), dma((2,)),
             dma((nz + low,)), dma((nz + low,)), dma((nz + low,)), dma((nz + low,)),
-            dma((nz - 1,)), dma((nz - 1,)), dma((2,)), dma((2,)),
+            dma((nz,)), dma((nz,)), dma((2,)), dma((2,)),
         ],
         compiler_params=pltpu.CompilerParams(collective_id=0, has_side_effects=True),
     )(embeddings, fine_centroids, parents.reshape(1, local), coarse_centroids)

time: 88.8 us -> 78.1 us (0.88)
  Pallas kernels: 84.5 us -> 73.8 us
    pallas_call x1, Pallas kernels: 84.5 us -> 73.8 us  [fused_step(): pl.pallas_call(functools.partial(step_kernel, n, nz), out_shape=(jax.Shap...]
where the time goes in v2:
time: 78.1 us; the launch traced here: 77.9 us
  Pallas kernels  73.8 us (94%)
  local copies, waits for them, and re-layouts  3.45 us (4%)
    pallas_call x1, Pallas kernels, fused_step(): pl.pallas_call(functools.partial(step_kernel, n, nz), out_shape=(jax.Shap...  73.8 us
    unnamed x4, local copies, waits for them, and re-layouts  3.45 us

profile of v2, /device:TPU:0, one launch (start us, length us, event | category | flops | bytes accessed | tf_op | source)
XLA Modules:
  0.0 77.9 jit_solution(6214434457976021649)
XLA Ops:
  0.6 73.8 %shard_map.59 = (f32[512,768]{1,0:T(8,128)}, f32[128,768]{1,0:T(8,128)}) custom-call(bf16[128,768]{1,0:T(8,128)(2,1)} %emb.1, f32[512,768]{1,0:T(8,128)} %fine.1, s32[1,512]{1,0:T(1,128)} %bitcast.1, f32[128,768]{1,0:T(8,128)} %coarse.1), custom_call_target="tpu_custom_call" | custom-call | tf_op jit(solution)/shard_map/pallas_call | solution.py:430
  74.4 0.0 copy-start
  74.4 2.7 %copy.8 = f32[512,768]{1,0:T(8,128)} copy(f32[512,768]{1,0:T(8,128)} %get-tuple-element.4) | data formatting | bytes 3145728
  77.1 0.0 copy-done
  77.1 0.7 copy.9
Async XLA Ops:
  74.4 2.7 %copy-start = (f32[128,768]{1,0:T(8,128)S(1)}, f32[128,768]{1,0:T(8,128)}, u32[]{:S(2)}) copy-start(f32[128,768]{1,0:T(8,128)} %get-tuple-element.5) | copy-start | bytes 1179652

commit v3 on v2

--- a/solution.py
+++ b/solution.py
@@ -110,12 +110,13 @@
 
 
 def step_kernel(
-    n, nz, emb, fine, par, coarse, nf, nc,
-    G, narrow, pr, wh, wl, st, ss, sr, cs, cr, hi, lo,
+    n, nz, emb, fine_hbm, par, coarse, nf_hbm, nc,
+    fine, nf, acc,
+    G, narrow, pr, wh, st, ss, sr, cs, cr, hi, lo,
     xs, xr, ys, yr, zs, zr, own, ms, mr,
     g_recv, gz_send, gx_send, gy_send, st_send, st_recv,
     sum_send, sum_recv, cnt_sem, nf_send, nf_recv,
-    x_send, x_recv, y_send, y_recv, z_send, z_recv, m_sem, nc_sem,
+    x_send, x_recv, y_send, y_recv, z_send, z_recv, m_sem, nc_sem, load_sem, store_sem,
 ):
     d = lax.axis_index("dp")
     c = lax.axis_index("cent")
@@ -131,10 +132,27 @@
     other = 1 - d
 
     barrier = pltpu.get_barrier_semaphore()
-    for k in range(1, n):
-        pl.semaphore_signal(barrier, inc=1, device_id=(d, (c + k) % n), device_id_type=MESH)
-    pl.semaphore_signal(barrier, inc=1, device_id=(other, c), device_id_type=MESH)
-    pl.semaphore_wait(barrier, n)
+
+    def greet(core, chip):
+        pl.semaphore_signal(barrier, inc=1, device_id=(core, chip), device_id_type=MESH)
+
+    fine_in = pltpu.make_async_copy(fine_hbm, fine, load_sem.at[0])
+    emb_in = pltpu.make_async_copy(emb, G.at[xy * nz + z], load_sem.at[1])
+    greet(d, nbr_x)
+    greet(d, nbr_y)
+    greet(other, c)
+
+    @pl.when(z > 0)
+    def _():
+        greet(d, c - 4)
+
+    @pl.when(z < nz - 1)
+    def _():
+        greet(d, c + 4)
+
+    fine_in.start()
+    emb_in.start()
+    pl.semaphore_wait(barrier, 3 + jnp.where(z > 0, 1, 0) + jnp.where(z < nz - 1, 1, 0))
 
     def copy(src, dst, send, recv, core, chip):
         return pltpu.make_async_remote_copy(
@@ -188,7 +206,7 @@
         send_along(src, mine, h, gz_send.at[2 + h], z - 1)
         send_piece(src, mine, h, gx_send.at[h], nbr_x)
         send_piece(src, mine, h, gy_send.at[h], nbr_y)
-    G[mine] = emb[...]
+    fine_in.wait()
     narrow[...] = fine[...].astype(jnp.bfloat16)
     half_norm = 0.5 * jnp.sum(fine[...] * fine[...], axis=1, keepdims=True)
 
@@ -222,27 +240,34 @@
             send_piece(block, slot, h, gx_send.at[2 * i + h], nbr_x)
             send_piece(block, slot, h, gy_send.at[2 * i + h], nbr_y)
 
+    def relay_y(i):
+        slot = cols[1] * nz + order[i]
+        for h in range(2):
+            send_piece(piece_of(slot, h), slot, h, gy_send.at[2 * (nz + i) + h], nbr_y)
+
     def forward_sides(i):
         o = order[i]
         for h in range(2):
-            for r in (1, 2):
-                arrived(cols[r] * nz + o, h)
-            if i < low:
-                slot = cols[1] * nz + o
-                send_piece(piece_of(slot, h), slot, h, gy_send.at[2 * (nz + i) + h], nbr_y)
-            else:
-                slot = cols[2] * nz + o
-                send_piece(piece_of(slot, h), slot, h, gx_send.at[2 * (nz + i - low) + h], nbr_x)
-
+            for r in (2, 1):
+                slot = cols[r] * nz + o
+                arrived(slot, h)
+                if r == 2 and i >= low:
+                    send = gx_send.at[2 * (nz + i - low) + h]
+                    send_piece(piece_of(slot, h), slot, h, send, nbr_x)
+
+    emb_in.wait()
     block_logits(0, 0)
     for i in range(1, nz):
         forward_column(i)
+        if i == nz - 1:
+            for t in range(low):
+                relay_y(t)
         forward_sides(i - 1)
         block_logits(0, i)
         block_logits(1, i - 1)
         block_logits(2, i - 1)
+    forward_sides(nz - 1)
     send_stats(0)
-    forward_sides(nz - 1)
     for r in (1, 2):
         block_logits(r, nz - 1)
         send_stats(r)
@@ -252,8 +277,7 @@
         block_logits(3, i)
     send_stats(3)
 
-    counts = jnp.zeros((local, 1), jnp.float32)
-    for r in range(4):
+    def column_weights(r, counts):
         col = cols[r]
         pltpu.make_async_copy(
             st.at[col, pl.ds(1, n - 1)], st.at[col, pl.ds(1, n - 1)], st_recv.at[col]
@@ -265,34 +289,38 @@
         factor = jnp.exp(peaks[0] - top) / total
         for t in range(nz):
             lanes = slice(t * rows, (t + 1) * rows)
-            soft = pr[r, :, lanes] * factor[t:t + 1, :]
-            counts = counts + jnp.sum(soft, axis=1, keepdims=True)
-            high = soft.astype(jnp.bfloat16)
-            wh[r, :, lanes] = high
-            wl[r, :, lanes] = (soft - high.astype(jnp.float32)).astype(jnp.bfloat16)
-    cs[...] = to_row(counts)
-    count_copy = copy(cs, cr, cnt_sem.at[0], cnt_sem.at[1], other, c)
-    count_copy.start()
+            soft = (pr[r, :, lanes] * factor[t:t + 1, :]).astype(jnp.bfloat16)
+            wh[r, :, lanes] = soft
+            counts = counts + soft.astype(jnp.float32)
+        return counts
 
     own_cols = pl.ds(pl.multiple_of(d * half, 128), half)
     other_cols = pl.ds(pl.multiple_of(other * half, 128), half)
     part = local // 2
 
-    def sums(h, columns):
-        picked = pl.ds(h * part, part)
-        out = jnp.zeros((part, half), jnp.float32)
-        for r in range(4):
-            block = G[pl.ds(cols[r] * nz, nz), :, columns].reshape(nz * rows, half)
-            out = out + dot(wh[r, picked, :], block) + dot(wl[r, picked, :], block)
-        return out
-
+    def column_sums(r, h, columns):
+        block = G[pl.ds(cols[r] * nz, nz), :, columns].reshape(nz * rows, half)
+        return dot(wh[r, pl.ds(h * part, part), :], block)
+
+    spread = jnp.zeros((local, rows), jnp.float32)
+    for r in range(3):
+        spread = column_weights(r, spread)
+    for side, columns in enumerate((other_cols, own_cols)):
+        for h in range(2):
+            acc[side, h] = (
+                column_sums(0, h, columns) + column_sums(1, h, columns)
+            ) + column_sums(2, h, columns)
+    spread = column_weights(3, spread)
     sum_copies = []
     for h in range(2):
-        ss[h] = sums(h, other_cols)
+        ss[h] = acc[0, h] + column_sums(3, h, other_cols)
         one = copy(ss.at[h], sr.at[h], sum_send.at[h], sum_recv.at[h], other, c)
         one.start()
         sum_copies.append(one)
-    own_sums = [sums(h, own_cols) for h in range(2)]
+    cs[...] = to_row(jnp.sum(spread, axis=1, keepdims=True))
+    count_copy = copy(cs, cr, cnt_sem.at[0], cnt_sem.at[1], other, c)
+    count_copy.start()
+    own_sums = [acc[1, h] + column_sums(3, h, own_cols) for h in range(2)]
 
     count_copy.wait()
     mass_row = 1.0 + (cs[...] + cr[...])
@@ -362,6 +390,13 @@
         send_x(i, close + yr[nz + t].astype(jnp.float32))
     for i in range(nz):
         own[i] = partial(0, i)
+    stores = []
+    for h in range(2):
+        nf_copies[h].wait_recv()
+        picked = pl.ds(h * part, part)
+        one = pltpu.make_async_copy(nf.at[picked], nf_hbm.at[picked], store_sem.at[h])
+        one.start()
+        stores.append(one)
     for k in range(1, n):
         to = (c + k) % n
         copy(ms.at[to], mr.at[n - k], m_sem.at[0], m_sem.at[1], d, to).start()
@@ -411,6 +446,8 @@
         x_copy(i).wait_send()
         y_copy(i).wait_send()
     for one in nf_copies:
+        one.wait_send()
+    for one in stores:
         one.wait()
     last.wait()
 
@@ -424,6 +461,7 @@
     half = width // 2
     bf, f32 = jnp.bfloat16, jnp.float32
     vmem = pl.BlockSpec(memory_space=pltpu.VMEM)
+    hbm = pl.BlockSpec(memory_space=pl.ANY)
     dma = pltpu.SemaphoreType.DMA
     V = pltpu.VMEM
     block = (coarse_rows, half)
@@ -433,13 +471,15 @@
             jax.ShapeDtypeStruct(fine_centroids.shape, f32),
             jax.ShapeDtypeStruct(coarse_centroids.shape, f32),
         ),
-        in_specs=[vmem] * 4,
-        out_specs=(vmem, vmem),
+        in_specs=[hbm, hbm, vmem, vmem],
+        out_specs=(hbm, vmem),
         scratch_shapes=[
+            V((local, width), f32),
+            V((local, width), f32),
+            V((2, 2, local // 2, half), f32),
             V((n, rows, width), bf),
             V((local, width), bf),
             V((4, local, nz * rows), f32),
-            V((4, local, nz * rows), bf),
             V((4, local, nz * rows), bf),
             V((4, n, 2 * nz, rows), f32),
             V((2, local // 2, half), f32),
@@ -461,7 +501,7 @@
             dma((4,)), dma((4,)),
             dma((2,)), dma((2,)), dma((2,)), dma((2,)), dma((2,)),
             dma((nz + low,)), dma((nz + low,)), dma((nz + low,)), dma((nz + low,)),
-            dma((nz,)), dma((nz,)), dma((2,)), dma((2,)),
+            dma((nz,)), dma((nz,)), dma((2,)), dma((2,)), dma((2,)), dma((2,)),
         ],
         compiler_params=pltpu.CompilerParams(collective_id=0, has_side_effects=True),
     )(embeddings, fine_centroids, parents.reshape(1, local), coarse_centroids)

time: 78.1 us -> 75.1 us (0.962)
  Pallas kernels: 73.8 us -> 70.8 us
    pallas_call x1, Pallas kernels: 73.8 us -> 70.8 us  [fused_step(): pl.pallas_call(functools.partial(step_kernel, n, nz), out_shape=(jax.Shap...]
where the time goes in v3:
time: 75.1 us; the launch traced here: 74.9 us
  Pallas kernels  70.8 us (94%)
  local copies, waits for them, and re-layouts  3.45 us (5%)
    pallas_call x1, Pallas kernels, fused_step(): pl.pallas_call(functools.partial(step_kernel, n, nz), out_shape=(jax.Shap...  70.8 us
    unnamed x4, local copies, waits for them, and re-layouts  3.45 us

profile of v3, /device:TPU:0, one launch (start us, length us, event | category | flops | bytes accessed | tf_op | source)
XLA Modules:
  0.0 74.9 jit_solution(1667895757487399038)
XLA Ops:
  0.6 70.8 %shard_map.59 = (f32[512,768]{1,0:T(8,128)}, f32[128,768]{1,0:T(8,128)}) custom-call(bf16[128,768]{1,0:T(8,128)(2,1)} %emb.1, f32[512,768]{1,0:T(8,128)} %fine_hbm.1, s32[1,512]{1,0:T(1,128)} %bitcast.1, f32[128,768]{1,0:T(8,128)} %coarse.1), custom_call_target="tpu_custom_call" | custom-call | tf_op jit(solution)/shard_map/pallas_call | solution.py:468
  71.4 0.0 copy-start
  71.4 2.7 %copy.8 = f32[512,768]{1,0:T(8,128)} copy(f32[512,768]{1,0:T(8,128)} %get-tuple-element.4) | data formatting | bytes 3145728
  74.1 0.0 copy-done
  74.1 0.7 copy.9
Async XLA Ops:
  71.4 2.7 %copy-start = (f32[128,768]{1,0:T(8,128)S(1)}, f32[128,768]{1,0:T(8,128)}, u32[]{:S(2)}) copy-start(f32[128,768]{1,0:T(8,128)} %get-tuple-element.5) | copy-start | bytes 1179652
